TPU v7x, 256 devices: a whole 4x4x8 slice. The times are simulated.
256 devices in a mesh: ctx: 64 (over z, y, core), tp: 4 (over x).
Axes of the slice: x: 4, y: 4, z: 8, core: 2. Of those that a mesh axis runs over, the one named last changes fastest.
Arguments:
- projected: bfloat16 [8192, 4, 4640], P('ctx', 'tp'), may hold values from -6 to 6
- conv_weight: float32 [4, 4, 2560], P('tp'), may hold values from -3 to 3
- conv_bias: float32 [4, 2560], P('tp'), may hold values from -1.5 to 1.5
- step_bias: float32 [4, 32], P('tp'), may hold values from -1 to 0.5
- log_rates: float32 [4, 32], P('tp'), as said below
- norm_gain: float32 [4, 2048], P('tp'), may hold values from 0.1 to 1.9
- out_weight: bfloat16 [4, 2048, 4096], P('tp', 'ctx'), may hold values from -0.0625 to 0.0625
Outputs:
- mixed: bfloat16 [8192, 4096], P('ctx', 'tp')
Inputs may be any that keep to these rules, and one draw needn't show every extreme that they name: log_rates lies between log(0.3 / 8192) and log(1 / 25).
All inputs are finite; a program needn't handle non-finite values.
Results may differ from a plain program's by a relative error of at most 0.0058.
Values may be sent and summed in bfloat16 or wider, within the bound.
No kernel may reach another device: no remote copies, remote signals or barrier semaphores. Data moves between devices by JAX's collectives and lax.ppermute only.
A program may use at most 320 MiB of HBM per device.

v0:
```python
import jax
import jax.numpy as jnp
import numpy as np
from jax import lax
from jax.sharding import PartitionSpec as P

P_SIZE = 64
N = 256
KCONV = 4
SPAN = 128
GCH = 2048
GCONV = 2560
highest_precision = lax.Precision.HIGHEST


def from_behind(shard, axis, by):
    peers = lax.axis_size(axis)
    pairs = [(i, i + by) for i in range(peers) if 0 <= i + by < peers]
    return lax.ppermute(shard, axis, pairs)


def ssd_blocks(inputs_x, step_sizes, decay_rate, b_keys, c_keys, block_rows):
    row_count = inputs_x.shape[0]
    block_count = row_count // block_rows
    head_count = inputs_x.shape[1]
    head_width = inputs_x.shape[2]
    state_count = b_keys.shape[1]
    x_blocks = inputs_x.reshape(block_count, block_rows, head_count, head_width)
    step_blocks = step_sizes.reshape(block_count, block_rows, head_count)
    b_blocks = b_keys.reshape(block_count, block_rows, state_count)
    c_blocks = c_keys.reshape(block_count, block_rows, state_count)
    causal_mask = (jnp.arange(block_rows)[:, None] >= jnp.arange(block_rows)[None, :])[None]

    def advance(carried, pieces):
        x_block, step_block, b_block, c_block = pieces
        log_steps = step_block * decay_rate[None, :]
        running = jnp.cumsum(log_steps, axis=0)
        intersection = jnp.dot(c_block, b_block.T, preferred_element_type=jnp.float32)
        b_float = b_block.astype(jnp.float32)
        c_float = c_block.astype(jnp.float32)
        log_gaps = running.T[:, :, None] - running.T[:, None, :]
        factors = jnp.where(causal_mask, jnp.exp(jnp.where(causal_mask, log_gaps, 0.0)), 0.0)
        factors = factors * intersection[None] * step_block.T[:, None, :]
        within = jnp.einsum("hts,shp->thp", factors, x_block, precision=highest_precision)
        carried_part = (
            jnp.einsum("tn,hpn->thp", c_float, carried, precision=highest_precision)
            * jnp.exp(running)[:, :, None]
        )
        tail_weight = jnp.exp(running[-1][None, :] - running) * step_block
        weighted = x_block * tail_weight[:, :, None]
        updated = carried * jnp.exp(running[-1])[:, None, None] + jnp.einsum(
            "shp,sn->hpn", weighted, b_float, precision=highest_precision
        )
        return (updated, within + carried_part)

    initial = jnp.zeros((head_count, head_width, state_count), jnp.float32)
    final_state, outputs = lax.scan(advance, initial, (x_blocks, step_blocks, b_blocks, c_blocks))
    total_log = jnp.sum(step_sizes * decay_rate[None, :], axis=0)
    return (outputs.reshape(row_count, head_count, head_width), final_state, total_log)


def on_device(projected, conv_weight, conv_bias, step_bias, log_rates, norm_gain, out_weight):
    row_count = projected.shape[0]
    conv_input = projected[:, :, GCH : GCH + GCONV]
    rim_rows = from_behind(conv_input[row_count - (KCONV - 1) :], "ctx", 1)
    padded = jnp.concatenate([rim_rows, conv_input], axis=0).astype(jnp.float32)
    mixed_conv = conv_bias[None]
    for offset in range(KCONV):
        mixed_conv = mixed_conv + conv_weight[:, offset][None] * padded[offset : offset + row_count]
    activated = jax.nn.silu(mixed_conv).astype(jnp.bfloat16)
    values = activated[:, :, :GCH]
    key_rows = activated[:, :, GCH:]
    raw_steps = projected[:, :, GCH + GCONV :]
    decay_rate = -jnp.exp(log_rates)
    devices = lax.axis_size("ctx")
    shard_width = GCH // devices
    shard_heads = max(1, shard_width // P_SIZE)
    piece_width = shard_width // shard_heads
    head_table = (
        np.arange(devices)[:, None] * shard_width // P_SIZE + np.arange(shard_heads)[None, :]
    ).reshape(-1)
    spread_steps = jnp.take(raw_steps, jnp.asarray(head_table, jnp.int32), axis=2)
    local_values, local_steps = (
        lax.all_to_all(values, "ctx", split_axis=2, concat_axis=0, tiled=True),
        lax.all_to_all(spread_steps, "ctx", split_axis=2, concat_axis=0, tiled=True),
    )
    all_keys = lax.all_gather(key_rows, "ctx", axis=0, tiled=True)
    sequence = local_values.shape[0]
    first_head = lax.axis_index("ctx") * shard_width // P_SIZE
    bias_slice = lax.dynamic_slice_in_dim(step_bias[0], first_head, shard_heads)
    rate_slice = lax.dynamic_slice_in_dim(decay_rate[0], first_head, shard_heads)
    step_sizes = jax.nn.softplus(local_steps[:, 0].astype(jnp.float32) + bias_slice[None, :])
    outputs, final_state, total_log = ssd_blocks(
        local_values[:, 0].astype(jnp.float32).reshape(sequence, shard_heads, piece_width),
        step_sizes,
        rate_slice,
        all_keys[:, 0, :N],
        all_keys[:, 0, N:],
        4 * SPAN,
    )
    pieces_out = [outputs.reshape(sequence, shard_width).astype(jnp.bfloat16)]
    scanned = lax.all_to_all(
        jnp.stack(pieces_out, axis=1), "ctx", split_axis=0, concat_axis=2, tiled=True
    )
    gated = scanned.astype(jnp.float32) * jax.nn.silu(projected[:, :, :GCH].astype(jnp.float32))
    normed = (
        gated * lax.rsqrt(jnp.mean(gated * gated, axis=2, keepdims=True) + 1e-05) * norm_gain[None]
    ).astype(jnp.bfloat16)
    summed = jnp.einsum(
        "tgr,grd->td",
        normed,
        lax.all_gather(out_weight, "ctx", axis=1, tiled=True),
        preferred_element_type=jnp.float32,
    )
    shares = lax.psum_scatter(summed, "tp", scatter_dimension=1, tiled=True)
    return shares.astype(jnp.bfloat16)


def solution(mesh):
    return jax.shard_map(
        on_device,
        mesh=mesh,
        in_specs=(
            P("ctx", "tp", None),
            P("tp", None, None),
            P("tp", None),
            P("tp", None),
            P("tp", None),
            P("tp", None),
            P("tp", "ctx", None),
        ),
        out_specs=P("ctx", "tp"),
        check_vma=False,
    )
```

profile of v0, /device:TPU:1, one launch (start us, length us, event | category | flops | bytes accessed | tf_op | source)
XLA Modules:
  0.0 387.9 jit_solution(16653090227472884516)
XLA Ops:
  6.5 1.4 slice.62
  8.2 4.7 %collective-permute-start = (bf16[3,1,2560]{2,0,1:T(4,128)(2,1)S(1)}, bf16[3,1,2560]{2,0,1:T(4,128)(2,1)S(1)}, u32[]{:S(2)}, u32[]{:S(2)}) collective-permute-start(bf16[3,1,2560]{2,0,1:T(4,128)(2,1)S(1)} %copy.77), channel_id=1, source_target_pairs={{0,4},{4,8},{8,12},{12,16},{16,20},{20,24},{24,28},{28,32},{32,36}... | collective-permute-start | bytes 46088 | tf_op jit(solution)/shard_map/ppermute | solution.py:19
  16.9 13.5 %all-to-all-start = ((bf16[128,1,64]{0,1,2:T(2,128)(2,1)}), bf16[128,1,64]{0,1,2:T(2,128)(2,1)S(1)}, u32[]{:S(2)}, u32[]{:S(2)}) async-start(bf16[128,1,64]{0,1,2:T(2,128)(2,1)} %copy.66), calls=%async_computation | async-start | bytes 65536 | tf_op jit(solution)/shard_map/all_to_all | solution.py:85
  31.7 11.5 %reduce.12 = bf16[2048,128]{1,0:T(8,128)(2,1)S(1)} reduce(bf16[2048,1,128]{2,1,0:T(2,128)(2,1)S(1)} %bitcast.163, bf16[]{:T(256)} %broadcast.159), dimensions={1}, to_apply=%bitcast.98.reduce_sub_computation | reduce | bytes 1048578
  44.2 10.3 %all-to-all-start.1 = ((bf16[64,2,2048]{2,1,0:T(2,128)(2,1)}), bf16[64,2,2048]{2,1,0:T(2,128)(2,1)S(1)}, u32[]{:S(2)}, u32[]{:S(2)}) async-start(bf16[64,2,2048]{2,1,0:T(2,128)(2,1)} %reshape.445), calls=%async_computation.1 | async-start | bytes 1048576 | tf_op jit(solution)/shard_map/all_to_all | solution.py:84
  57.5 14.9 %all-to-all-done.1 = bf16[64,2,2048]{2,1,0:T(2,128)(2,1)S(1)} async-done(((bf16[64,2,2048]{2,1,0:T(2,128)(2,1)}), bf16[64,2,2048]{2,1,0:T(2,128)(2,1)S(1)}, u32[]{:S(2)}, u32[]{:S(2)}) %all-to-all-start.1) | async-done | bytes 524320 | tf_op jit(solution)/shard_map/all_to_all | solution.py:84
  74.1 2.7 copy.70
  76.8 26.9 %all-gather.3.cloned.1.call-done = bf16[8192,1,512]{2,0,1:T(8,128)(2,1)} async-done(((bf16[128,1,512]{2,0,1:T(8,128)(2,1)}), bf16[8192,1,512]{2,0,1:T(8,128)(2,1)}) %all-gather.3.cloned.1.call-update) | async-done | bytes 8388624 | tf_op jit(solution)/shard_map/all_gather | solution.py:87
  103.7 5.9 %fusion.41 = (bf16[8192,1,256]{2,0,1:T(8,128)(2,1)}, bf16[8192,1,256]{2,0,1:T(8,128)(2,1)}) fusion(bf16[8192,1,512]{2,0,1:T(8,128)(2,1)} %all-gather.3.cloned.1.call-done), kind=kLoop, calls=%fused_computation.76 | loop fusion | bytes 16777216 | tf_op jit(solution)/shard_map/slice | solution.py:98
  109.6 184.8 %while.14 = (s32[]{:T(128)}, f32[1,32,256]{2,1,0:T(8,128)S(1)}, bf16[16,512,1,32]{1,3,2,0:T(8,128)(2,1)S(1)}, f32[16,512,1]{1,0,2:T(8,128)S(1)}, f32[1]{0:T(128)...) while((s32[]{:T(128)}, f32[1,32,256]{2,1,0:T(8,128)S(1)}, ...), condition=%wide.region_3.4_spmd.clone.clone, body=%wide.region_0.0_spmd.clone.clone.sunk | while | flops 337266176 | bytes 4002620 | solution.py:57
  113.5 2.4 broadcast_multiply_fusion.2
  115.9 1.4 fusion.69
  125.0 2.4 broadcast_multiply_fusion.2
  127.4 1.4 fusion.69
  136.5 2.4 broadcast_multiply_fusion.2
  139.0 1.4 fusion.69
  148.1 2.4 broadcast_multiply_fusion.2
  150.5 1.4 fusion.69
  154.3 1.4 fusion.67
  159.7 2.5 broadcast_multiply_fusion.2
  162.1 1.4 fusion.69
  166.0 1.4 fusion.67
  171.3 2.4 broadcast_multiply_fusion.2
  182.8 2.4 broadcast_multiply_fusion.2
  185.3 1.4 fusion.69
  194.4 2.4 broadcast_multiply_fusion.2
  206.0 2.4 broadcast_multiply_fusion.2
  217.5 2.4 broadcast_multiply_fusion.2
  229.1 2.4 broadcast_multiply_fusion.2
  240.6 2.4 broadcast_multiply_fusion.2
  243.0 1.4 fusion.69
  252.1 2.4 broadcast_multiply_fusion.2
  254.6 1.4 fusion.69
  263.7 2.4 broadcast_multiply_fusion.2
  266.1 1.4 fusion.69
  275.2 2.4 broadcast_multiply_fusion.2
  277.6 1.4 fusion.69
  286.7 2.4 broadcast_multiply_fusion.2
  289.1 1.4 fusion.69
  294.4 1.7 reduce.13
  296.0 1.9 copy.81
  298.0 2.8 reshape.447
  300.8 23.8 %all_to_all.12 = bf16[64,2,2048]{2,1,0:T(2,128)(2,1)S(1)} all-to-all(bf16[64,2,2048]{2,1,0:T(2,128)(2,1)} %reshape.447), channel_id=1, replica_groups=mesh['ctx'=64,'tp'=4] {'ctx'}, dimensions={0} | all-to-all | bytes 1048576 | tf_op jit(solution)/shard_map/all_to_all | solution.py:102
  324.6 7.1 %reshape.448 = bf16[8192,1,32]{2,1,0:T(2,128)(2,1)} reshape(bf16[64,2,2048]{2,1,0:T(2,128)(2,1)S(1)} %all_to_all.12) | data formatting | bytes 1048576
  331.8 8.0 %copy.74 = bf16[8192,1,32]{0,2,1:T(8,128)(2,1)S(1)} copy(bf16[8192,1,32]{2,1,0:T(2,128)(2,1)} %reshape.448) | data formatting | bytes 1048576 | tf_op jit(solution)/shard_map/all_to_all | solution.py:102
  341.3 9.6 %fusion.25 = f32[128,4096]{1,0:T(8,128)} fusion(bf16[1,2048,4096]{2,1,0:T(8,128)(2,1)} %all-gather.5.cloned.1.call-done, f32[128,1,2048]{0,2,1:T(8,128)S(1)} %get-tuple-element.150, f32[2048]{0:T(1024)S(1)} %bitcast.173, f32[128]{0:T(128)S(1)} %add_rsqrt_fusion), kind=kOutput, calls=%fused_computation.38 | convolution fusion | flops 2148270080 | bytes 19931648 | tf_op jit(solution)/shard_map/tgr,grd->td/dot_general | solution.py:109
  350.9 28.7 %reduce-scatter.2.cloned.1.call-done = f32[128,1024]{1,0:T(8,128)} async-done(((f32[128,4096]{1,0:T(8,128)}), f32[128,1024]{1,0:T(8,128)}) %reduce-scatter.2.cloned.1.call-update) | async-done | bytes 524304 | tf_op jit(solution)/shard_map/reduce_scatter | solution.py:115
  379.6 1.8 convert_element_type.107
  (271 shorter events, 118.4 us)
Async XLA Ops:
  6.5 49.0 %copy-start = (f32[1,32]{1,0:T(1,128)S(1)}, f32[1,32]{1,0:T(1,128)}, u32[]{:S(2)}) copy-start(f32[1,32]{1,0:T(1,128)} %param.13) | copy-start | bytes 388
  6.5 6.4 %copy-start.5 = (f32[1,4,2560]{2,1,0:T(4,128)S(1)}, f32[1,4,2560]{2,1,0:T(4,128)}, u32[]{:S(2)}) copy-start(f32[1,4,2560]{2,1,0:T(4,128)} %param.11) | copy-start | bytes 122884
  6.5 6.5 %slice-start = ((bf16[128,1,4640]{0,2,1:T(8,128)(2,1)}), bf16[128,1,2560]{0,2,1:T(8,128)(2,1)S(1)}, s32[]{:S(2)}) async-start(bf16[128,1,4640]{0,2,1:T(8,128)(2,1)} %param.10), calls=%async_computation.7 | async-start | bytes 1310720 | tf_op jit(solution)/shard_map/slice | solution.py:64
  6.5 97.2 %all-gather.3.cloned.1.call-start = ((), (), s32[]{:S(2)}) async-start(), calls=%async_computation.4 | async-start | bytes 8519680 | tf_op jit(solution)/shard_map/all_gather | solution.py:87
  8.2 5.1 %copy-start.6 = (f32[1,2560]{1,0:T(1,128)S(1)}, f32[1,2560]{1,0:T(1,128)}, u32[]{:S(2)}) copy-start(f32[1,2560]{1,0:T(1,128)} %param.12) | copy-start | bytes 30724
  8.2 5.6 %collective-permute-start = (bf16[3,1,2560]{2,0,1:T(4,128)(2,1)S(1)}, bf16[3,1,2560]{2,0,1:T(4,128)(2,1)S(1)}, u32[]{:S(2)}, u32[]{:S(2)}) collective-permute-start(bf16[3,1,2560]{2,0,1:T(4,128)(2,1)S(1)} %copy.77), channel_id=1, source_target_pairs={{0,4},{4,8},{8,12},{12,16},{16,20},{20,24},{24,28},{28,32},{32,36}... | collective-permute-start | bytes 46088 | tf_op jit(solution)/shard_map/ppermute | solution.py:19
  14.0 1.6 copy-start.7
  14.0 1.6 copy-start.2
  16.9 27.3 %all-to-all-start = ((bf16[128,1,64]{0,1,2:T(2,128)(2,1)}), bf16[128,1,64]{0,1,2:T(2,128)(2,1)S(1)}, u32[]{:S(2)}, u32[]{:S(2)}) async-start(bf16[128,1,64]{0,1,2:T(2,128)(2,1)} %copy.66), calls=%async_computation | async-start | bytes 65536 | tf_op jit(solution)/shard_map/all_to_all | solution.py:85
  43.2 13.0 %copy-start.8 = (f32[1,32]{1,0:T(1,128)S(1)}, f32[1,32]{1,0:T(1,128)}, u32[]{:S(2)}) copy-start(f32[1,32]{1,0:T(1,128)} %param.14) | copy-start | bytes 388
  44.2 28.2 %all-to-all-start.1 = ((bf16[64,2,2048]{2,1,0:T(2,128)(2,1)}), bf16[64,2,2048]{2,1,0:T(2,128)(2,1)S(1)}, u32[]{:S(2)}, u32[]{:S(2)}) async-start(bf16[64,2,2048]{2,1,0:T(2,128)(2,1)} %reshape.445), calls=%async_computation.1 | async-start | bytes 1048576 | tf_op jit(solution)/shard_map/all_to_all | solution.py:84
  54.5 286.5 %all-gather.5.cloned.1.call-start = ((), (), s32[]{:S(2)}) async-start(), calls=%async_computation.5 | async-start | bytes 17039360 | tf_op jit(solution)/shard_map/all_gather | solution.py:112
  55.3 324.3 %reduce-scatter.2.cloned.1.call-start = ((), (), s32[]{:S(2)}) async-start(), calls=%async_computation.6 | async-start | bytes 2621440 | tf_op jit(solution)/shard_map/reduce_scatter | solution.py:115
  76.8 32.8 %copy-start.3 = (bf16[16,512,1,32]{1,3,2,0:T(8,128)(2,1)S(1)}, bf16[16,512,1,32]{1,3,2,0:T(8,128)(2,1)}, u32[]{:S(2)}) copy-start(bf16[16,512,1,32]{1,3,2,0:T(8,128)(2,1)} %custom-call.3) | copy-start | bytes 1572868
  340.6 0.7 copy-start.4
  350.9 30.5 %copy-start.1 = (f32[1,32]{1,0:T(1,128)S(1)}, f32[1,32]{1,0:T(1,128)}, u32[]{:S(2)}) copy-start(f32[1,32]{1,0:T(1,128)} %param.13) | copy-start | bytes 388
Sparse Core Ops, SparseCore 0:
  15.7 87.9 all-gather.2
  106.5 97.1 all-gather.4
  351.1 28.4 reduce-scatter.1
where the time goes:
time: 391 us; the launch traced here: 388 us
  matrix products  91.8 us (23%)
  other arithmetic  75.4 us (19%)
  waiting for transfers between devices  71.7 us (18%)
  local copies, waits for them, and re-layouts  60.7 us (16%)
  starting transfers between devices  28.7 us (7%)
  blocking collectives  23.8 us (6%)
  loops' own time  22.3 us (6%)
  between operations  13.4 us (3%)
    mul x16, other arithmetic, advance(): weighted = x_block * tail_weight[:, :, None]  38.7 us
    reduce_scatter x1, waiting for transfers between devices, on_device(): shares = lax.psum_scatter(summed, 'tp', scatter_dimension=1, tiled=True)  28.7 us
    all_gather x1, waiting for transfers between devices, on_device(): all_keys = lax.all_gather(key_rows, 'ctx', axis=0, tiled=True)  26.9 us
    all_to_all x1, blocking collectives, on_device(): lax.all_to_all(jnp.stack(pieces_out, axis=1), 'ctx', split_axis=0, concat...  23.8 us
    another operation x1, loops' own time, ssd_blocks(): lax.scan(advance, initial, (x_blocks, step_blocks, b_blocks, c_blocks))  22.3 us
    dot_general x16, matrix products, advance(): jnp.dot(c_block, b_block.T, preferred_element_type=jnp.float32)  22 us
    dot_general x16, matrix products, advance(): jnp.einsum('shp,sn->hpn', weighted, b_float, precision=highest_precision)  21.3 us
    dot_general x16, matrix products, advance(): jnp.einsum('tn,hpn->thp', c_float, carried, precision=highest_precision)  20.8 us
  transfers between devices with their start and end apart: 6, of which 4 were waited for; matrix products, arithmetic and copies ran while one was open for 55% of the time, Pallas kernels for 0%

commit v1 on v0

--- a/solution.py
+++ b/solution.py
@@ -84,7 +84,10 @@
         lax.all_to_all(values, "ctx", split_axis=2, concat_axis=0, tiled=True),
         lax.all_to_all(spread_steps, "ctx", split_axis=2, concat_axis=0, tiled=True),
     )
-    all_keys = lax.all_gather(key_rows, "ctx", axis=0, tiled=True)
+    treat_desk = lambda array_here, array_axis: jnp.concatenate(
+        lax.all_to_all(jnp.stack([array_here] * lax.psum(1, "ctx")), "ctx", 0, 0), axis=array_axis
+    )
+    all_keys = treat_desk(key_rows, 0)
     sequence = local_values.shape[0]
     first_head = lax.axis_index("ctx") * shard_width // P_SIZE
     bias_slice = lax.dynamic_slice_in_dim(step_bias[0], first_head, shard_heads)

time: 391 us -> 604 us (1.54)
  waiting for transfers between devices: 71.7 us -> 272 us
  starting transfers between devices: 28.7 us -> 35 us
    all_to_all x0 -> x1, waiting for transfers between devices: none -> 225 us  [on_device(): lax.all_to_all(jnp.stack([array_here] * lax.psum(1, 'ctx')), 'ctx', 0, 0)]
    all_gather x1 -> x0, waiting for transfers between devices: 26.9 us -> none  [on_device(): all_keys = lax.all_gather(key_rows, 'ctx', axis=0, tiled=True)]
    all_to_all x0 -> x1, starting transfers between devices: none -> 6.04 us  [on_device(): lax.all_to_all(jnp.stack([array_here] * lax.psum(1, 'ctx')), 'ctx', 0, 0)]
    unnamed x27 -> x23, local copies, waits for them, and re-layouts: 14.9 us -> 13.9 us
  transfers between devices with their start and end apart: 6 -> 6, of which waited for: 4 -> 4; matrix products, arithmetic and copies ran while one was open for 55% -> 35% of each run, Pallas kernels for 0% -> 0%
where the time goes in v1:
time: 604 us; the launch traced here: 601 us
  waiting for transfers between devices  272 us (45%)
  matrix products  91.5 us (15%)
  other arithmetic  75.2 us (12%)
  local copies, waits for them, and re-layouts  64.8 us (11%)
  starting transfers between devices  35 us (6%)
  blocking collectives  26.5 us (4%)
  loops' own time  22 us (4%)
  between operations  13.7 us (2%)
    all_to_all x1, waiting for transfers between devices, on_device(): lax.all_to_all(jnp.stack([array_here] * lax.psum(1, 'ctx')), 'ctx', 0, 0)  225 us
    mul x16, other arithmetic, advance(): weighted = x_block * tail_weight[:, :, None]  38.6 us
    reduce_scatter x1, waiting for transfers between devices, on_device(): shares = lax.psum_scatter(summed, 'tp', scatter_dimension=1, tiled=True)  28.8 us
    all_to_all x1, blocking collectives, on_device(): lax.all_to_all(jnp.stack(pieces_out, axis=1), 'ctx', split_axis=0, concat...  26.5 us
    another operation x1, loops' own time, ssd_blocks(): lax.scan(advance, initial, (x_blocks, step_blocks, b_blocks, c_blocks))  22 us
    dot_general x16, matrix products, advance(): jnp.dot(c_block, b_block.T, preferred_element_type=jnp.float32)  22 us
    dot_general x16, matrix products, advance(): jnp.einsum('shp,sn->hpn', weighted, b_float, precision=highest_precision)  21.2 us
    dot_general x16, matrix products, advance(): jnp.einsum('tn,hpn->thp', c_float, carried, precision=highest_precision)  20.6 us
  transfers between devices with their start and end apart: 6, of which 4 were waited for; matrix products, arithmetic and copies ran while one was open for 35% of the time, Pallas kernels for 0%

profile of v1, /device:TPU:1, one launch (start us, length us, event | category | flops | bytes accessed | tf_op | source)
XLA Modules:
  0.0 601.1 jit_solution(12963521938681404211)
XLA Ops:
  9.2 13.2 %all-to-all-start = ((bf16[128,1,64]{0,1,2:T(2,128)(2,1)}), bf16[128,1,64]{0,1,2:T(2,128)(2,1)S(1)}, u32[]{:S(2)}, u32[]{:S(2)}) async-start(bf16[128,1,64]{0,1,2:T(2,128)(2,1)} %copy.62), calls=%async_computation | async-start | bytes 65536 | tf_op jit(solution)/shard_map/all_to_all | solution.py:85
  22.4 1.4 slice.64
  24.0 3.7 collective-permute-start
  31.0 11.5 %reduce.12 = bf16[2048,128]{1,0:T(8,128)(2,1)S(1)} reduce(bf16[2048,1,128]{2,1,0:T(2,128)(2,1)S(1)} %bitcast.166, bf16[]{:T(256)} %broadcast.162), dimensions={1}, to_apply=%bitcast.101.reduce_sub_computation | reduce | bytes 1048578
  43.4 11.9 %all-to-all-start.1 = ((bf16[64,2,2048]{2,1,0:T(2,128)(2,1)}), bf16[64,2,2048]{2,1,0:T(2,128)(2,1)S(1)}, u32[]{:S(2)}, u32[]{:S(2)}) async-start(bf16[64,2,2048]{2,1,0:T(2,128)(2,1)} %reshape.452), calls=%async_computation.1 | async-start | bytes 1048576 | tf_op jit(solution)/shard_map/all_to_all | solution.py:84
  55.3 17.7 %all-to-all-done.1 = bf16[64,2,2048]{2,1,0:T(2,128)(2,1)S(1)} async-done(((bf16[64,2,2048]{2,1,0:T(2,128)(2,1)}), bf16[64,2,2048]{2,1,0:T(2,128)(2,1)S(1)}, u32[]{:S(2)}, u32[]{:S(2)}) %all-to-all-start.1) | async-done | bytes 524320 | tf_op jit(solution)/shard_map/all_to_all | solution.py:84
  73.0 4.2 stack.2
  77.2 6.0 %all-to-all-start.2 = ((bf16[64,128,1,512]{3,1,2,0:T(8,128)(2,1)}), bf16[64,128,1,512]{3,1,2,0:T(8,128)(2,1)}, u32[]{:S(2)}, u32[]{:S(2)}) async-start(bf16[64,128,1,512]{3,1,2,0:T(8,128)(2,1)} %stack.2), calls=%async_computation.2 | async-start | bytes 16777216 | tf_op jit(solution)/shard_map/all_to_all | solution.py:88
  88.0 2.7 copy.66
  90.7 224.7 %all-to-all-done.2 = bf16[64,128,1,512]{3,1,2,0:T(8,128)(2,1)} async-done(((bf16[64,128,1,512]{3,1,2,0:T(8,128)(2,1)}), bf16[64,128,1,512]{3,1,2,0:T(8,128)(2,1)}, u32[]{:S(2)}, u32[]{:S(2)}) %all-to-all-start.2) | async-done | bytes 8388640 | tf_op jit(solution)/shard_map/all_to_all | solution.py:88
  315.4 5.7 fusion.41
  321.1 184.8 %while.14 = (s32[]{:T(128)}, f32[1,32,256]{2,1,0:T(8,128)S(1)}, bf16[16,512,1,32]{1,3,2,0:T(8,128)(2,1)S(1)}, f32[16,512,1]{1,0,2:T(8,128)S(1)}, f32[1]{0:T(128)...) while((s32[]{:T(128)}, f32[1,32,256]{2,1,0:T(8,128)S(1)}, ...), condition=%wide.region_3.4_spmd.clone.clone, body=%wide.region_0.0_spmd.clone.clone.sunk | while | flops 337266176 | bytes 4002620 | solution.py:57
  325.0 2.4 broadcast_multiply_fusion.2
  327.5 1.4 fusion.69
  336.6 2.4 broadcast_multiply_fusion.2
  339.0 1.4 fusion.69
  348.2 2.4 broadcast_multiply_fusion.2
  350.6 1.4 fusion.69
  359.7 2.4 broadcast_multiply_fusion.2
  362.1 1.4 fusion.69
  371.3 2.4 broadcast_multiply_fusion.2
  373.7 1.4 fusion.69
  382.8 2.4 broadcast_multiply_fusion.2
  385.2 1.4 fusion.69
  394.4 2.4 broadcast_multiply_fusion.2
  396.8 1.4 fusion.69
  405.9 2.4 broadcast_multiply_fusion.2
  408.3 1.4 fusion.69
  417.5 2.4 broadcast_multiply_fusion.2
  419.9 1.4 fusion.69
  429.0 2.4 broadcast_multiply_fusion.2
  431.5 1.4 fusion.69
  440.6 2.4 broadcast_multiply_fusion.2
  452.1 2.4 broadcast_multiply_fusion.2
  454.6 1.4 fusion.69
  463.7 2.4 broadcast_multiply_fusion.2
  466.1 1.4 fusion.69
  475.2 2.4 broadcast_multiply_fusion.2
  477.7 1.4 fusion.69
  486.8 2.4 broadcast_multiply_fusion.2
  498.3 2.4 broadcast_multiply_fusion.2
  508.1 2.1 reshape.454
  510.2 26.5 %all_to_all.32 = bf16[64,2,2048]{2,1,0:T(2,128)(2,1)S(1)} all-to-all(bf16[64,2,2048]{2,1,0:T(2,128)(2,1)S(1)} %reshape.454), channel_id=1, replica_groups=mesh['ctx'=64,'tp'=4] {'ctx'}, dimensions={0} | all-to-all | bytes 1048576 | tf_op jit(solution)/shard_map/all_to_all | solution.py:105
  536.7 7.1 %reshape.455 = bf16[8192,1,32]{2,1,0:T(2,128)(2,1)} reshape(bf16[64,2,2048]{2,1,0:T(2,128)(2,1)S(1)} %all_to_all.32) | data formatting | bytes 1048576
  543.9 8.0 %copy.70 = bf16[8192,1,32]{0,2,1:T(8,128)(2,1)S(1)} copy(bf16[8192,1,32]{2,1,0:T(2,128)(2,1)} %reshape.455) | data formatting | bytes 1048576 | tf_op jit(solution)/shard_map/all_to_all | solution.py:105
  554.1 9.6 %fusion.25 = f32[128,4096]{1,0:T(8,128)} fusion(bf16[1,2048,4096]{2,1,0:T(8,128)(2,1)} %all-gather.2.cloned.1.call-done, f32[128,1,2048]{0,2,1:T(8,128)S(1)} %get-tuple-element.142, f32[2048]{0:T(1024)S(1)} %bitcast.176, f32[128]{0:T(128)S(1)} %add_rsqrt_fusion), kind=kOutput, calls=%fused_computation.38 | convolution fusion | flops 2148270080 | bytes 19931648 | tf_op jit(solution)/shard_map/tgr,grd->td/dot_general | solution.py:112
  563.7 28.8 %reduce-scatter.2.cloned.1.call-done = f32[128,1024]{1,0:T(8,128)} async-done(((f32[128,4096]{1,0:T(8,128)}), f32[128,1024]{1,0:T(8,128)}) %reduce-scatter.2.cloned.1.call-update) | async-done | bytes 524304 | tf_op jit(solution)/shard_map/reduce_scatter | solution.py:118
  592.5 1.8 convert_element_type.107
  (267 shorter events, 122.3 us)
Async XLA Ops:
  6.5 77.7 %copy-start = (f32[1,32]{1,0:T(1,128)S(1)}, f32[1,32]{1,0:T(1,128)}, u32[]{:S(2)}) copy-start(f32[1,32]{1,0:T(1,128)} %param.13) | copy-start | bytes 388
  6.5 21.2 %copy-start.4 = (f32[1,4,2560]{2,1,0:T(4,128)S(1)}, f32[1,4,2560]{2,1,0:T(4,128)}, u32[]{:S(2)}) copy-start(f32[1,4,2560]{2,1,0:T(4,128)} %param.11) | copy-start | bytes 122884
  9.2 34.2 %all-to-all-start = ((bf16[128,1,64]{0,1,2:T(2,128)(2,1)}), bf16[128,1,64]{0,1,2:T(2,128)(2,1)S(1)}, u32[]{:S(2)}, u32[]{:S(2)}) async-start(bf16[128,1,64]{0,1,2:T(2,128)(2,1)} %copy.62), calls=%async_computation | async-start | bytes 65536 | tf_op jit(solution)/shard_map/all_to_all | solution.py:85
  22.4 5.5 slice-start
  24.0 4.1 copy-start.5
  24.0 4.6 collective-permute-start
  43.4 29.6 %all-to-all-start.1 = ((bf16[64,2,2048]{2,1,0:T(2,128)(2,1)}), bf16[64,2,2048]{2,1,0:T(2,128)(2,1)S(1)}, u32[]{:S(2)}, u32[]{:S(2)}) async-start(bf16[64,2,2048]{2,1,0:T(2,128)(2,1)} %reshape.452), calls=%async_computation.1 | async-start | bytes 1048576 | tf_op jit(solution)/shard_map/all_to_all | solution.py:84
  77.2 7.7 %copy-start.6 = (f32[1,32]{1,0:T(1,128)S(1)}, f32[1,32]{1,0:T(1,128)}, u32[]{:S(2)}) copy-start(f32[1,32]{1,0:T(1,128)} %param.14) | copy-start | bytes 388
  77.2 238.2 %all-to-all-start.2 = ((bf16[64,128,1,512]{3,1,2,0:T(8,128)(2,1)}), bf16[64,128,1,512]{3,1,2,0:T(8,128)(2,1)}, u32[]{:S(2)}, u32[]{:S(2)}) async-start(bf16[64,128,1,512]{3,1,2,0:T(8,128)(2,1)} %stack.2), calls=%async_computation.2 | async-start | bytes 16777216 | tf_op jit(solution)/shard_map/all_to_all | solution.py:88
  83.3 470.5 %all-gather.2.cloned.1.call-start = ((), (), s32[]{:S(2)}) async-start(), calls=%async_computation.5 | async-start | bytes 17039360 | tf_op jit(solution)/shard_map/all_gather | solution.py:115
  84.0 508.5 %reduce-scatter.2.cloned.1.call-start = ((), (), s32[]{:S(2)}) async-start(), calls=%async_computation.6 | async-start | bytes 2621440 | tf_op jit(solution)/shard_map/reduce_scatter | solution.py:118
  552.1 1.3 copy-start.2
  553.4 0.7 copy-start.3
  563.7 30.6 %copy-start.1 = (f32[1,32]{1,0:T(1,128)S(1)}, f32[1,32]{1,0:T(1,128)}, u32[]{:S(2)}) copy-start(f32[1,32]{1,0:T(1,128)} %param.13) | copy-start | bytes 388
Sparse Core Ops, SparseCore 0:
  86.9 222.1 all-gather.1
  563.8 28.6 reduce-scatter.1
